TPU v7x, 256 devices: a whole 4x4x8 slice. The times are simulated.
256 devices in a mesh: ia: 8 (over z_lo, core), ja: 32 (over y, x, z_hi).
Axes of the slice: x: 4, y: 4, z: 8 (z_hi: 2, z_lo: 4; z = z_hi * 4 + z_lo), core: 2. Of those that a mesh axis runs over, the one named last changes fastest.
Arguments:
- slab_rows: bfloat16 [256, 768, 128], P('ia', 'ja'), may hold values from -6 to 6
- column_rows: bfloat16 [512, 768, 128], P('ja', 'ia'), may hold values from -6 to 6
- pair_tile: bfloat16 [256, 512, 128], P('ia', 'ja'), may hold values from -6 to 6
- cotangent: bfloat16 [256, 512, 128], P('ia', 'ja'), may hold values from -6 to 6
- weights_left: bfloat16 [128, 256], replicated, may hold values from -0.5 to 0.5
- weights_right: bfloat16 [128, 256], replicated, may hold values from -0.5 to 0.5
- gate_weight: bfloat16 [128, 128], replicated, may hold values from -0.5 to 0.5
- out_weight: bfloat16 [128, 128], replicated, may hold values from -0.5 to 0.5
- input_gain: float32 [128], replicated, may hold values from 0.1 to 1.9
- input_bias: float32 [128], replicated, may hold values from -3 to 3
- update_gain: float32 [128], replicated, may hold values from 0.1 to 1.9
- update_bias: float32 [128], replicated, may hold values from -3 to 3
Outputs:
- update: bfloat16 [256, 512, 128], P('ia', 'ja')
- grad_slab: bfloat16 [256, 768, 128], P('ia', 'ja')
- grad_columns: bfloat16 [512, 768, 128], P('ja', 'ia')
- grad_tile: bfloat16 [256, 512, 128], P('ia', 'ja')
All inputs are finite; a program needn't handle non-finite values.
Results may differ from a plain program's by a relative error of at most 0.018.
Values may be sent and summed in bfloat16 or wider, within the bound.
No kernel may reach another device: no remote copies, remote signals or barrier semaphores. Data moves between devices by JAX's collectives and lax.ppermute only.
A program may use at most 128 MiB of HBM per device.

v0:
```python
import jax
import jax.numpy as jnp
from jax import lax
from jax.sharding import Mesh
from jax.sharding import PartitionSpec as P

JA = ("ja_0", "ja_1", "ja_2")
epsilon = 1e-05


def summed_rows(terms, axes):
    total = terms.astype(jnp.bfloat16)
    for axis in axes:
        total = lax.psum_scatter(total, axis, scatter_dimension=0, tiled=True)
    return total.astype(jnp.float32)


def in_blocks(array, dim, devices):
    before, after = (array.shape[:dim], array.shape[dim + 1 :])
    return jnp.moveaxis(array.reshape(*before, devices, -1, *after), dim, 0)


def sent_and_summed(array, axis, dim):
    devices = lax.axis_size(axis)
    blocks = lax.all_to_all(in_blocks(array, dim, devices), axis, 0, 0, tiled=True)
    return jnp.sum(blocks.astype(jnp.float32), axis=0)


def normalize(values, gain, bias):
    values = values.astype(jnp.float32)
    centre = jnp.mean(values, axis=-1, keepdims=True)
    shifted = values - centre
    inverse = lax.rsqrt(jnp.mean(shifted * shifted, axis=-1, keepdims=True) + epsilon)
    scaled = shifted * inverse
    return (scaled * gain + bias, scaled, inverse)


def norm_back(scaled, inverse, grad_out, gain):
    grad_hat = grad_out * gain
    first_mean = jnp.mean(grad_hat, axis=-1, keepdims=True)
    second_mean = jnp.mean(grad_hat * scaled, axis=-1, keepdims=True)
    return inverse * (grad_hat - first_mean - scaled * second_mean)


def project(rows, weights, input_gain, input_bias):
    normed, scaled, inverse = normalize(rows, input_gain, input_bias)
    hidden = jnp.dot(normed.astype(jnp.bfloat16), weights, preferred_element_type=jnp.float32)
    half_width = weights.shape[1] // 2
    linear = hidden[..., :half_width]
    sigma = jax.nn.sigmoid(hidden[..., half_width:])
    return ((sigma * linear).astype(jnp.bfloat16), linear, sigma, scaled, inverse)


def project_back(grad_edge, linear, sigma, scaled, inverse, weights, input_gain):
    joined = jnp.concatenate(
        [grad_edge * sigma, grad_edge * linear * sigma * (1.0 - sigma)], axis=-1
    )
    grad_norm = jnp.dot(joined.astype(jnp.bfloat16), weights.T, preferred_element_type=jnp.float32)
    return norm_back(scaled, inverse, grad_norm, input_gain).astype(jnp.bfloat16)


def shards(
    slab_rows,
    column_rows,
    pair_tile,
    cotangent,
    weights_left,
    weights_right,
    gate_weight,
    out_weight,
    input_gain,
    input_bias,
    update_gain,
    update_bias,
):
    left, lin_left, sig_left, scaled_left, inv_left = project(
        slab_rows, weights_left, input_gain, input_bias
    )
    right, lin_right, sig_right, scaled_right, inv_right = project(
        column_rows, weights_right, input_gain, input_bias
    )
    left_whole = lax.all_gather(left, JA, axis=1, tiled=True)
    panel_piece = lax.all_gather(right, "ia", axis=1, tiled=True)
    left_slice = left_whole
    running = jnp.einsum(
        "ikc,jkc->ijc", left_slice, panel_piece, preferred_element_type=jnp.float32
    )
    tri_norm, tri_scaled, tri_inverse = normalize(running, update_gain, update_bias)
    outer = jnp.dot(tri_norm.astype(jnp.bfloat16), out_weight, preferred_element_type=jnp.float32)
    tile_norm, tile_scaled, tile_inverse = normalize(pair_tile, input_gain, input_bias)
    gate_linear = jnp.dot(
        tile_norm.astype(jnp.bfloat16), gate_weight, preferred_element_type=jnp.float32
    )
    gate = jax.nn.sigmoid(gate_linear)
    update = (gate * outer).astype(jnp.bfloat16)
    grad_update = cotangent.astype(jnp.float32)
    grad_outer = (grad_update * gate).astype(jnp.bfloat16)
    grad_gate = (grad_update * outer * gate * (1.0 - gate)).astype(jnp.bfloat16)
    grad_tnorm = jnp.dot(grad_outer, out_weight.T, preferred_element_type=jnp.float32)
    grad_tri = norm_back(tri_scaled, tri_inverse, grad_tnorm, update_gain).astype(jnp.bfloat16)
    grad_pnorm = jnp.dot(grad_gate, gate_weight.T, preferred_element_type=jnp.float32)
    grad_tile = norm_back(tile_scaled, tile_inverse, grad_pnorm, input_gain).astype(jnp.bfloat16)
    left_sums = summed_rows(
        jnp.einsum("ijc,jkc->kic", grad_tri, panel_piece, preferred_element_type=jnp.float32), JA
    )
    left_slice = left_whole
    right_sums = sent_and_summed(
        jnp.einsum("ijc,ikc->kjc", grad_tri, left_slice, preferred_element_type=jnp.float32).astype(
            jnp.bfloat16
        ),
        "ia",
        0,
    )
    grad_left = jnp.transpose(left_sums, (1, 0, 2))
    grad_right = jnp.transpose(right_sums, (1, 0, 2))
    grad_slab = project_back(
        grad_left, lin_left, sig_left, scaled_left, inv_left, weights_left, input_gain
    )
    grad_columns = project_back(
        grad_right, lin_right, sig_right, scaled_right, inv_right, weights_right, input_gain
    )
    return (update, grad_slab, grad_columns, grad_tile)


def solution(mesh):
    finer = Mesh(mesh.devices.reshape(mesh.shape["ia"], 4, 4, 2), ("ia", "ja_0", "ja_1", "ja_2"))
    in_specs = (
        P("ia", JA, None),
        P(JA, "ia", None),
        P("ia", JA, None),
        P("ia", JA, None),
        P(),
        P(),
        P(),
        P(),
        P(),
        P(),
        P(),
        P(),
    )
    out_specs = (P("ia", JA, None), P("ia", JA, None), P(JA, "ia", None), P("ia", JA, None))
    return jax.shard_map(
        shards, mesh=finer, in_specs=in_specs, out_specs=out_specs, check_vma=False
    )
```

profile of v0, /device:TPU:1, one launch (start us, length us, event | category | flops | bytes accessed | tf_op | source)
XLA Modules:
  0.0 401.9 jit_solution(11439921015196536878)
XLA Ops:
  7.3 1.3 convert_reduce_fusion.1
  8.6 1.6 fusion.14
  10.2 1.6 fusion.37
  11.9 1.1 copy-done.1
  13.0 1.0 multiply_convert_fusion.1
  15.0 0.9 copy-done.5
  15.9 0.8 multiply_convert_fusion.2
  19.6 1.4 copy.77
  21.0 39.5 %all-gather.3.cloned.1.call-done = bf16[16,768,128]{2,1,0:T(8,128)(2,1)} async-done(((bf16[16,96,128]{2,1,0:T(8,128)(2,1)}), bf16[16,768,128]{2,1,0:T(8,128)(2,1)}) %all-gather.3.cloned.1.call-update) | async-done | bytes 3145744 | tf_op jit(solution)/shard_map/all_gather | solution.py:83
  60.6 3.9 copy.74
  64.5 137.4 %all-gather.5.cloned.1.call-done = bf16[32,768,128]{2,1,0:T(8,128)(2,1)} async-done(((bf16[32,24,128]{2,1,0:T(8,128)(2,1)}), bf16[32,768,128]{2,1,0:T(8,128)(2,1)}) %all-gather.5.cloned.1.call-update) | async-done | bytes 6291472 | tf_op jit(solution)/shard_map/all_gather | solution.py:82
  201.9 41.8 %copy.75 = bf16[32,768,128]{0,1,2:T(8,128)(2,1)} copy(bf16[32,768,128]{2,1,0:T(8,128)(2,1)} %all-gather.5.cloned.1.call-done) | data formatting | bytes 12582912 | tf_op jit(solution)/shard_map/all_gather | solution.py:82
  243.7 10.1 %fusion.99 = (f32[32,16]{0,1:T(8,128)S(1)}, f32[32,16,128]{0,1,2:T(8,128)S(1)}) fusion(bf16[16,768,128]{1,0,2:T(8,128)(2,1)S(1)} %copy.74, bf16[32,768,128]{0,1,2:T(8,128)(2,1)} %copy.75), kind=kOutput, calls=%fused_computation.142 | convolution fusion | flops 100728320 | bytes 9701376 | tf_op jit(solution)/shard_map/ikc,jkc->ijc/dot_general | solution.py:85
  254.5 1.3 multiply_convert_fusion
  255.8 0.8 copy-done.4
  256.6 4.6 %convert_bitcast_fusion = bf16[768,32,128]{0,1,2:T(8,128)(2,1)} fusion(bf16[16,768,128]{1,0,2:T(8,128)(2,1)S(1)} %copy.74, bf16[32,16,128]{0,1,2:T(8,128)(2,1)S(1)} %get-tuple-element.14), kind=kOutput, calls=%fused_computation.1 | convolution fusion | flops 103809024 | bytes 9568256 | tf_op jit(solution)/shard_map/ijc,jkc->kic/dot_general | solution.py:104
  261.1 9.6 %copy.79 = bf16[768,32,128]{2,1,0:T(8,128)(2,1)} copy(bf16[768,32,128]{0,1,2:T(8,128)(2,1)} %convert_bitcast_fusion) | data formatting | bytes 12582912 | tf_op jit(solution)/shard_map/convert_element_type | solution.py:12
  270.7 14.0 %convert_bitcast_fusion.1 = bf16[768,16,128]{0,1,2:T(8,128)(2,1)S(1)} fusion(bf16[32,768,128]{0,1,2:T(8,128)(2,1)} %copy.75, bf16[32,16,128]{0,1,2:T(8,128)(2,1)} %copy-done.4), kind=kOutput, calls=%fused_computation.2 | convolution fusion | flops 102236160 | bytes 9568256 | tf_op jit(solution)/shard_map/ijc,ikc->kjc/dot_general | solution.py:108
  284.7 4.0 copy.82
  288.7 6.5 %all-to-all-start = ((bf16[8,96,16,128]{3,2,1,0:T(8,128)(2,1)}), bf16[8,96,16,128]{3,2,1,0:T(8,128)(2,1)}, u32[]{:S(2)}, u32[]{:S(2)}) async-start(bf16[8,96,16,128]{3,2,1,0:T(8,128)(2,1)} %bitcast.75), calls=%async_computation.2 | async-start | bytes 6291456 | tf_op jit(solution)/shard_map/all_to_all | solution.py:25
  295.2 37.4 %reduce-scatter.6.cloned.1.call-done = bf16[192,32,128]{2,1,0:T(8,128)(2,1)} async-done(((bf16[768,32,128]{2,1,0:T(8,128)(2,1)}), bf16[192,32,128]{2,1,0:T(8,128)(2,1)}) %reduce-scatter.6.cloned.1.call-update) | async-done | bytes 1572880 | tf_op jit(solution)/shard_map/reduce_scatter | solution.py:14
  333.4 0.8 multiply_convert_fusion.3
  335.0 1.0 fusion.63
  336.0 29.9 %all-to-all-done = bf16[8,96,16,128]{3,2,1,0:T(8,128)(2,1)} async-done(((bf16[8,96,16,128]{3,2,1,0:T(8,128)(2,1)}), bf16[8,96,16,128]{3,2,1,0:T(8,128)(2,1)}, u32[]{:S(2)}, u32[]{:S(2)}) %all-to-all-start) | async-done | bytes 3145760 | tf_op jit(solution)/shard_map/all_to_all | solution.py:25
  365.9 2.4 convert_reduce_fusion
  368.4 1.1 fusion.21
  369.5 2.0 copy.97
  371.6 2.1 fusion.96
  373.6 1.7 fusion.13
  375.3 17.2 %reduce-scatter.10.cloned.1.call-done = bf16[24,4096]{1,0:T(8,128)(2,1)} async-done(((bf16[48,4096]{1,0:T(8,128)(2,1)}), bf16[24,4096]{1,0:T(8,128)(2,1)}) %reduce-scatter.10.cloned.1.call-update) | async-done | bytes 196624
  392.5 1.1 fusion.45
  394.2 1.2 fusion.35
  (117 shorter events, 6.6 us)
Async XLA Ops:
  7.2 7.4 %copy-start.31 = (f32[128]{0:T(128)S(1)}, f32[128]{0:T(128)}, u32[]{:S(2)}) copy-start(f32[128]{0:T(128)} %param.20) | copy-start | bytes 1540
  7.2 7.4 %copy-start.34 = (f32[128]{0:T(128)S(1)}, f32[128]{0:T(128)}, u32[]{:S(2)}) copy-start(f32[128]{0:T(128)} %param.21) | copy-start | bytes 1540
  7.2 6.8 %copy-start.8 = (bf16[32,24,128]{2,1,0:T(8,128)(2,1)S(1)}, bf16[32,24,128]{2,1,0:T(8,128)(2,1)}, u32[]{:S(2)}) copy-start(bf16[32,24,128]{2,1,0:T(8,128)(2,1)} %param.12) | copy-start | bytes 589828
  7.2 7.4 %copy-start.27 = (bf16[128,256]{1,0:T(8,128)(2,1)S(1)}, bf16[128,256]{1,0:T(8,128)(2,1)}, u32[]{:S(2)}) copy-start(bf16[128,256]{1,0:T(8,128)(2,1)} %param.16) | copy-start | bytes 196612
  7.2 53.3 %all-gather.3.cloned.1.call-start = ((), (), s32[]{:S(2)}) async-start(), calls=%async_computation.4 | async-start | bytes 3538944 | tf_op jit(solution)/shard_map/all_gather | solution.py:83
  10.2 6.8 %copy-start.12 = (bf16[32,16,128]{2,1,0:T(8,128)(2,1)S(1)}, bf16[32,16,128]{2,1,0:T(8,128)(2,1)}, u32[]{:S(2)}) copy-start(bf16[32,16,128]{2,1,0:T(8,128)(2,1)} %param.14) | copy-start | bytes 393220
  13.0 5.3 %copy-start.29 = (bf16[128,128]{1,0:T(8,128)(2,1)S(1)}, bf16[128,128]{1,0:T(8,128)(2,1)}, u32[]{:S(2)}) copy-start(bf16[128,128]{1,0:T(8,128)(2,1)} %param.18) | copy-start | bytes 98308
  13.0 6.4 %copy-start.13 = (bf16[32,16,128]{2,1,0:T(8,128)(2,1)S(1)}, bf16[32,16,128]{2,1,0:T(8,128)(2,1)}, u32[]{:S(2)}) copy-start(bf16[32,16,128]{2,1,0:T(8,128)(2,1)} %param.15) | copy-start | bytes 393220
  13.0 6.4 %copy-start.23 = (bf16[128,128]{1,0:T(8,128)(2,1)S(1)}, bf16[128,128]{1,0:T(8,128)(2,1)}, u32[]{:S(2)}) copy-start(bf16[128,128]{1,0:T(8,128)(2,1)} %param.19) | copy-start | bytes 98308
  14.0 187.9 %all-gather.5.cloned.1.call-start = ((), (), s32[]{:S(2)}) async-start(), calls=%async_computation.5 | async-start | bytes 6488064 | tf_op jit(solution)/shard_map/all_gather | solution.py:82
  14.2 6.8 %copy-start.15 = (f32[32,24]{1,0:T(8,128)}, f32[32,24]{1,0:T(8,128)S(1)}, u32[]{:S(2)}) copy-start(f32[32,24]{1,0:T(8,128)S(1)} %broadcast_multiply_fusion.2) | copy-start | bytes 9220
  14.6 6.4 %copy-start.19 = (f32[32,24]{1,0:T(8,128)}, f32[32,24]{1,0:T(8,128)S(1)}, u32[]{:S(2)}) copy-start(f32[32,24]{1,0:T(8,128)S(1)} %add_rsqrt_fusion) | copy-start | bytes 9220
  16.8 315.8 %reduce-scatter.6.cloned.1.call-start = ((), (), s32[]{:S(2)}) async-start(), calls=%async_computation.6 | async-start | bytes 7864320 | tf_op jit(solution)/shard_map/reduce_scatter | solution.py:14
  243.7 10.4 %copy-start.3 = (f32[32,16,128]{0,1,2:T(8,128)S(1)}, f32[32,16,128]{0,1,2:T(8,128)}, u32[]{:S(2)}) copy-start(f32[32,16,128]{0,1,2:T(8,128)} %copy.77) | copy-start | bytes 786436
  243.7 10.4 %copy-start.35 = (f32[128]{0:T(128)S(1)}, f32[128]{0:T(128)}, u32[]{:S(2)}) copy-start(f32[128]{0:T(128)} %param.22) | copy-start | bytes 1540
  288.7 44.2 %copy-start.11 = (bf16[32,16,128]{0,1,2:T(8,128)(2,1)S(1)}, bf16[32,16,128]{0,1,2:T(8,128)(2,1)}, u32[]{:S(2)}) copy-start(bf16[32,16,128]{0,1,2:T(8,128)(2,1)} %get-tuple-element.15) | copy-start | bytes 393220
  288.7 44.8 %copy-start.10 = (f32[32,16,128]{2,1,0:T(8,128)S(1)}, f32[32,16,128]{2,1,0:T(8,128)}, u32[]{:S(2)}) copy-start(f32[32,16,128]{2,1,0:T(8,128)} %copy-done.9) | copy-start | bytes 786436
  288.7 44.8 %copy-start.24 = (bf16[128,128]{1,0:T(8,128)(2,1)S(1)}, bf16[128,128]{1,0:T(8,128)(2,1)}, u32[]{:S(2)}) copy-start(bf16[128,128]{1,0:T(8,128)(2,1)} %param.19) | copy-start | bytes 98308
  288.7 45.6 %copy-start.14 = (bf16[32,16,128]{2,1,0:T(8,128)(2,1)S(1)}, bf16[32,16,128]{2,1,0:T(8,128)(2,1)}, u32[]{:S(2)}) copy-start(bf16[32,16,128]{2,1,0:T(8,128)(2,1)} %param.15) | copy-start | bytes 393220
  288.7 45.6 %copy-start.18 = (f32[32,16]{1,0:T(8,128)S(1)}, f32[32,16]{1,0:T(8,128)}, u32[]{:S(2)}) copy-start(f32[32,16]{1,0:T(8,128)} %copy-done.17) | copy-start | bytes 6148
  288.7 45.6 %copy-start.30 = (bf16[128,128]{1,0:T(8,128)(2,1)S(1)}, bf16[128,128]{1,0:T(8,128)(2,1)}, u32[]{:S(2)}) copy-start(bf16[128,128]{1,0:T(8,128)(2,1)} %param.18) | copy-start | bytes 98308
  288.7 45.6 %copy-start.32 = (f32[128]{0:T(128)S(1)}, f32[128]{0:T(128)}, u32[]{:S(2)}) copy-start(f32[128]{0:T(128)} %param.20) | copy-start | bytes 1540
  288.7 77.2 %all-to-all-start = ((bf16[8,96,16,128]{3,2,1,0:T(8,128)(2,1)}), bf16[8,96,16,128]{3,2,1,0:T(8,128)(2,1)}, u32[]{:S(2)}, u32[]{:S(2)}) async-start(bf16[8,96,16,128]{3,2,1,0:T(8,128)(2,1)} %bitcast.75), calls=%async_computation.2 | async-start | bytes 6291456 | tf_op jit(solution)/shard_map/all_to_all | solution.py:25
  295.2 74.3 %reduce-scatter.8.cloned.1.call-start = ((), (), s32[]{:S(2)}) async-start(), calls=%async_computation.7 | async-start | bytes 1966080 | tf_op jit(solution)/shard_map/reduce_scatter | solution.py:14
  332.6 59.9 %reduce-scatter.10.cloned.1.call-start = ((), (), s32[]{:S(2)}) async-start(), calls=%async_computation.8 | async-start | bytes 589824
  333.4 34.9 %copy-start.2 = (f32[16,96,256]{2,1,0:T(8,128)S(1)}, f32[16,96,256]{2,1,0:T(8,128)}, u32[]{:S(2)}) copy-start(f32[16,96,256]{2,1,0:T(8,128)} %copy-done.1) | copy-start | bytes 4718596
  368.3 3.2 copy-start.7
  368.3 3.2 copy-start.22
  369.5 23.0 %copy-start.6 = (f32[32,24,256]{2,1,0:T(8,128)S(1)}, f32[32,24,256]{2,1,0:T(8,128)}, u32[]{:S(2)}) copy-start(f32[32,24,256]{2,1,0:T(8,128)} %copy-done.5) | copy-start | bytes 2359300
  371.5 22.1 %copy-start.16 = (f32[32,24]{1,0:T(8,128)S(1)}, f32[32,24]{1,0:T(8,128)}, u32[]{:S(2)}) copy-start(f32[32,24]{1,0:T(8,128)} %copy-done.15) | copy-start | bytes 9220
  371.5 22.2 %copy-start.20 = (f32[32,24]{1,0:T(8,128)S(1)}, f32[32,24]{1,0:T(8,128)}, u32[]{:S(2)}) copy-start(f32[32,24]{1,0:T(8,128)} %copy-done.19) | copy-start | bytes 9220
  371.5 22.2 %copy-start.28 = (bf16[128,256]{1,0:T(8,128)(2,1)S(1)}, bf16[128,256]{1,0:T(8,128)(2,1)}, u32[]{:S(2)}) copy-start(bf16[128,256]{1,0:T(8,128)(2,1)} %param.16) | copy-start | bytes 196612
  (11 other events, 17.5 us)
Sparse Core Ops, SparseCore 0:
  14.1 46.4 all-gather.2
  64.3 137.5 all-gather.4
  270.8 61.7 reduce-scatter.5
  335.0 27.1 reduce-scatter.7
  371.6 20.8 reduce-scatter.9
where the time goes:
time: 403 us; the launch traced here: 402 us
  waiting for transfers between devices  262 us (65%)
  local copies, waits for them, and re-layouts  68.1 us (17%)
  matrix products  35.1 us (9%)
  other arithmetic  15.8 us (4%)
  between operations  14.3 us (4%)
  starting transfers between devices  7.09 us (2%)
    all_gather x1, waiting for transfers between devices, shards(): left_whole = lax.all_gather(left, JA, axis=1, tiled=True)  137 us
    all_gather x1, local copies, waits for them, and re-layouts, shards(): left_whole = lax.all_gather(left, JA, axis=1, tiled=True)  41.8 us
    all_gather x1, waiting for transfers between devices, shards(): panel_piece = lax.all_gather(right, 'ia', axis=1, tiled=True)  39.5 us
    reduce_scatter x2, waiting for transfers between devices, summed_rows(): total = lax.psum_scatter(total, axis, scatter_dimension=0, tiled=True)  37.4 us
    all_to_all x1, waiting for transfers between devices, sent_and_summed(): lax.all_to_all(in_blocks(array, dim, devices), axis, 0, 0, tiled=True)  29.9 us
    unnamed x6, waiting for transfers between devices  17.3 us
    dot_general x1, matrix products, shards(): jnp.einsum('ijc,ikc->kjc', grad_tri, left_slice, preferred_element_type=j...  14 us
    dot_general x1, matrix products, shards(): jnp.einsum('ikc,jkc->ijc', left_slice, panel_piece, preferred_element_typ...  10.1 us
  transfers between devices with their start and end apart: 6, of which 5 were waited for; matrix products, arithmetic and copies ran while one was open for 9% of the time, Pallas kernels for 0%

commit v1 on v0

--- a/solution.py
+++ b/solution.py
@@ -79,7 +79,15 @@
     right, lin_right, sig_right, scaled_right, inv_right = project(
         column_rows, weights_right, input_gain, input_bias
     )
-    left_whole = lax.all_gather(left, JA, axis=1, tiled=True)
+    left_whole = jnp.concatenate(
+        lax.all_to_all(
+            jnp.stack([left for _ in range(lax.psum(1, axis_name=JA))], 0),
+            axis_name=JA,
+            split_axis=0,
+            concat_axis=0,
+        ),
+        1,
+    )
     panel_piece = lax.all_gather(right, "ia", axis=1, tiled=True)
     left_slice = left_whole
     running = jnp.einsum(

time: 403 us -> 374 us (0.928)
  starting transfers between devices: 7.09 us -> 55.3 us
  waiting for transfers between devices: 262 us -> 225 us
  local copies, waits for them, and re-layouts: 68.1 us -> 45.4 us
  matrix products: 35.1 us -> 18.3 us
    all_gather x1 -> x0, waiting for transfers between devices: 137 us -> none  [shards(): left_whole = lax.all_gather(left, JA, axis=1, tiled=True)]
    all_gather x1, waiting for transfers between devices: 39.5 us -> 106 us  [shards(): panel_piece = lax.all_gather(right, 'ia', axis=1, tiled=True)]
    all_gather x1 -> x0, local copies, waits for them, and re-layouts: 41.8 us -> none  [shards(): left_whole = lax.all_gather(left, JA, axis=1, tiled=True)]
    all_to_all x1, starting transfers between devices: 6.53 us -> 40 us  [sent_and_summed(): lax.all_to_all(in_blocks(array, dim, devices), axis, 0, 0, tiled=True)]
    all_to_all x0 -> x1, waiting for transfers between devices: none -> 23.2 us  [shards(): lax.all_to_all(jnp.stack([left for _ in range(lax.psum(1, axis_name=JA))]...]
    all_to_all x0 -> x1, starting transfers between devices: none -> 14.7 us  [shards(): lax.all_to_all(jnp.stack([left for _ in range(lax.psum(1, axis_name=JA))]...]
    reduce_scatter x2, waiting for transfers between devices: 37.4 us -> 51.2 us  [summed_rows(): total = lax.psum_scatter(total, axis, scatter_dimension=0, tiled=True)]
    all_to_all x1, waiting for transfers between devices: 29.9 us -> 19.8 us  [sent_and_summed(): lax.all_to_all(in_blocks(array, dim, devices), axis, 0, 0, tiled=True)]
  transfers between devices with their start and end apart: 6 -> 6, of which waited for: 5 -> 6; matrix products, arithmetic and copies ran while one was open for 9% -> 7% of each run, Pallas kernels for 0% -> 0%
where the time goes in v1:
time: 374 us; the launch traced here: 373 us
  waiting for transfers between devices  225 us (60%)
  starting transfers between devices  55.3 us (15%)
  local copies, waits for them, and re-layouts  45.4 us (12%)
  matrix products  18.3 us (5%)
  other arithmetic  14.3 us (4%)
  between operations  14.2 us (4%)
    all_gather x1, waiting for transfers between devices, shards(): panel_piece = lax.all_gather(right, 'ia', axis=1, tiled=True)  106 us
    reduce_scatter x2, waiting for transfers between devices, summed_rows(): total = lax.psum_scatter(total, axis, scatter_dimension=0, tiled=True)  51.2 us
    all_to_all x1, starting transfers between devices, sent_and_summed(): lax.all_to_all(in_blocks(array, dim, devices), axis, 0, 0, tiled=True)  40 us
    unnamed x5, waiting for transfers between devices  25 us
    all_to_all x1, waiting for transfers between devices, shards(): lax.all_to_all(jnp.stack([left for _ in range(lax.psum(1, axis_name=JA))]...  23.2 us
    all_to_all x1, waiting for transfers between devices, sent_and_summed(): lax.all_to_all(in_blocks(array, dim, devices), axis, 0, 0, tiled=True)  19.8 us
    all_to_all x1, starting transfers between devices, shards(): lax.all_to_all(jnp.stack([left for _ in range(lax.psum(1, axis_name=JA))]...  14.7 us
    convert_element_type x1, local copies, waits for them, and re-layouts, summed_rows(): total = terms.astype(jnp.bfloat16)  9.69 us
  transfers between devices with their start and end apart: 6, of which 6 were waited for; matrix products, arithmetic and copies ran while one was open for 7% of the time, Pallas kernels for 0%

profile of v1, /device:TPU:1, one launch (start us, length us, event | category | flops | bytes accessed | tf_op | source)
XLA Modules:
  0.0 372.9 jit_solution(15406798128972139360)
XLA Ops:
  7.2 1.1 convert_reduce_fusion.2
  8.3 1.2 fusion.36
  9.6 1.4 fusion.69
  11.0 0.9 copy-done.4
  12.0 4.1 %stack.2 = bf16[32,32,24,128]{3,2,1,0:T(8,128)(2,1)} broadcast(bf16[32,24,128]{2,1,0:T(8,128)(2,1)S(1)} %multiply_convert_fusion.2), dimensions={1,2,3} | broadcast | bytes 6488064 | tf_op jit(solution)/shard_map/stack | solution.py:84
  16.1 14.7 %all-to-all-start = ((bf16[32,32,24,128]{3,2,1,0:T(8,128)(2,1)}), bf16[32,32,24,128]{3,2,1,0:T(8,128)(2,1)}, u32[]{:S(2)}, u32[]{:S(2)}) async-start(bf16[32,32,24,128]{3,2,1,0:T(8,128)(2,1)} %stack.2), calls=%async_computation | async-start | bytes 12582912 | tf_op jit(solution)/shard_map/all_to_all | solution.py:83
  32.4 1.2 copy-done.1
  33.5 1.0 multiply_convert_fusion.1
  36.0 1.4 copy.79
  37.5 106.3 %all-gather.2.cloned.1.call-done = bf16[16,768,128]{2,1,0:T(8,128)(2,1)} async-done(((bf16[16,96,128]{2,1,0:T(8,128)(2,1)}), bf16[16,768,128]{2,1,0:T(8,128)(2,1)}) %all-gather.2.cloned.1.call-update) | async-done | bytes 3145744 | tf_op jit(solution)/shard_map/all_gather | solution.py:91
  143.7 3.9 %copy.76 = bf16[16,768,128]{1,0,2:T(8,128)(2,1)S(1)} copy(bf16[16,768,128]{2,1,0:T(8,128)(2,1)} %all-gather.2.cloned.1.call-done) | data formatting | bytes 6291456 | tf_op jit(solution)/shard_map/all_gather | solution.py:91
  147.7 23.2 %all-to-all-done = bf16[32,32,24,128]{3,2,1,0:T(8,128)(2,1)} async-done(((bf16[32,32,24,128]{3,2,1,0:T(8,128)(2,1)}), bf16[32,32,24,128]{3,2,1,0:T(8,128)(2,1)}, u32[]{:S(2)}, u32[]{:S(2)}) %all-to-all-start) | async-done | bytes 6291488 | tf_op jit(solution)/shard_map/all_to_all | solution.py:83
  170.9 7.2 %copy.75 = bf16[32,32,24,128]{3,2,0,1:T(8,128)(2,1)} copy(bf16[32,32,24,128]{3,2,1,0:T(8,128)(2,1)} %all-to-all-done) | data formatting | bytes 12582912 | tf_op jit(solution)/shard_map/all_to_all | solution.py:83
  178.1 9.0 %copy.77 = bf16[32,768,128]{1,0,2:T(8,128)(2,1)} copy(bf16[32,768,128]{2,1,0:T(8,128)(2,1)} %bitcast.78) | data formatting | bytes 12582912 | tf_op jit(solution)/shard_map/reshape | solution.py:82
  187.1 4.6 %fusion.99 = (f32[32,16]{0,1:T(8,128)S(1)}, f32[32,16,128]{0,1,2:T(8,128)S(1)}) fusion(bf16[16,768,128]{1,0,2:T(8,128)(2,1)S(1)} %copy.76, bf16[32,768,128]{1,0,2:T(8,128)(2,1)} %copy.77), kind=kOutput, calls=%fused_computation.142 | convolution fusion | flops 100728320 | bytes 9701376 | tf_op jit(solution)/shard_map/ikc,jkc->ijc/dot_general | solution.py:93
  192.4 1.2 multiply_convert_fusion
  194.5 4.4 %convert_bitcast_fusion = bf16[768,32,128]{0,1,2:T(8,128)(2,1)} fusion(bf16[16,768,128]{1,0,2:T(8,128)(2,1)S(1)} %copy.76, bf16[32,16,128]{0,1,2:T(8,128)(2,1)S(1)} %get-tuple-element.14), kind=kOutput, calls=%fused_computation.1 | convolution fusion | flops 103809024 | bytes 9568256 | tf_op jit(solution)/shard_map/ijc,jkc->kic/dot_general | solution.py:112
  198.9 9.7 %copy.81 = bf16[768,32,128]{2,1,0:T(8,128)(2,1)} copy(bf16[768,32,128]{0,1,2:T(8,128)(2,1)} %convert_bitcast_fusion) | data formatting | bytes 12582912 | tf_op jit(solution)/shard_map/convert_element_type | solution.py:12
  208.6 3.9 %convert_bitcast_fusion.1 = bf16[768,16,128]{0,1,2:T(8,128)(2,1)S(1)} fusion(bf16[32,16,128]{0,1,2:T(8,128)(2,1)} %copy-done.8, bf16[32,768,128]{1,0,2:T(8,128)(2,1)} %copy.77), kind=kOutput, calls=%fused_computation.2 | convolution fusion | flops 102236160 | bytes 9568256 | tf_op jit(solution)/shard_map/ijc,ikc->kjc/dot_general | solution.py:116
  212.6 4.0 %copy.84 = bf16[768,16,128]{2,1,0:T(8,128)(2,1)} copy(bf16[768,16,128]{0,1,2:T(8,128)(2,1)S(1)} %convert_bitcast_fusion.1) | data formatting | bytes 6291456 | tf_op jit(solution)/shard_map/convert_element_type | solution.py:116
  216.6 40.0 %all-to-all-start.1 = ((bf16[8,96,16,128]{3,2,1,0:T(8,128)(2,1)}), bf16[8,96,16,128]{3,2,1,0:T(8,128)(2,1)}, u32[]{:S(2)}, u32[]{:S(2)}) async-start(bf16[8,96,16,128]{3,2,1,0:T(8,128)(2,1)} %bitcast.79), calls=%async_computation.3 | async-start | bytes 6291456 | tf_op jit(solution)/shard_map/all_to_all | solution.py:25
  256.6 47.5 %reduce-scatter.6.cloned.1.call-done = bf16[192,32,128]{2,1,0:T(8,128)(2,1)} async-done(((bf16[768,32,128]{2,1,0:T(8,128)(2,1)}), bf16[192,32,128]{2,1,0:T(8,128)(2,1)}) %reduce-scatter.6.cloned.1.call-update) | async-done | bytes 1572880 | tf_op jit(solution)/shard_map/reduce_scatter | solution.py:14
  306.5 1.0 fusion.63
  307.5 19.8 %all-to-all-done.1 = bf16[8,96,16,128]{3,2,1,0:T(8,128)(2,1)} async-done(((bf16[8,96,16,128]{3,2,1,0:T(8,128)(2,1)}), bf16[8,96,16,128]{3,2,1,0:T(8,128)(2,1)}, u32[]{:S(2)}, u32[]{:S(2)}) %all-to-all-start.1) | async-done | bytes 3145760 | tf_op jit(solution)/shard_map/all_to_all | solution.py:25
  327.3 2.4 convert_reduce_fusion
  330.2 3.6 reduce-scatter.8.cloned.1.call-done
  333.9 1.9 copy.99
  335.8 1.1 fusion.96
  336.9 1.7 fusion.13
  338.6 24.9 %reduce-scatter.10.cloned.1.call-done = bf16[24,4096]{1,0:T(8,128)(2,1)} async-done(((bf16[48,4096]{1,0:T(8,128)(2,1)}), bf16[24,4096]{1,0:T(8,128)(2,1)}) %reduce-scatter.10.cloned.1.call-update) | async-done | bytes 196624
  363.5 1.1 fusion.45
  365.2 1.2 fusion.35
  (94 shorter events, 7.9 us)
Async XLA Ops:
  7.2 24.5 %copy-start = (bf16[128,256]{1,0:T(8,128)(2,1)S(1)}, bf16[128,256]{1,0:T(8,128)(2,1)}, u32[]{:S(2)}) copy-start(bf16[128,256]{1,0:T(8,128)(2,1)} %param.17) | copy-start | bytes 196612
  11.0 0.9 copy-start.4
  16.1 14.8 %copy-start.6 = (bf16[16,96,128]{2,1,0:T(8,128)(2,1)S(1)}, bf16[16,96,128]{2,1,0:T(8,128)(2,1)}, u32[]{:S(2)}) copy-start(bf16[16,96,128]{2,1,0:T(8,128)(2,1)} %param.13) | copy-start | bytes 1179652
  16.1 15.7 %copy-start.20 = (f32[128]{0:T(128)S(1)}, f32[128]{0:T(128)}, u32[]{:S(2)}) copy-start(f32[128]{0:T(128)} %param.20) | copy-start | bytes 1540
  16.1 15.7 %copy-start.22 = (f32[128]{0:T(128)S(1)}, f32[128]{0:T(128)}, u32[]{:S(2)}) copy-start(f32[128]{0:T(128)} %param.21) | copy-start | bytes 1540
  16.1 154.8 %all-to-all-start = ((bf16[32,32,24,128]{3,2,1,0:T(8,128)(2,1)}), bf16[32,32,24,128]{3,2,1,0:T(8,128)(2,1)}, u32[]{:S(2)}, u32[]{:S(2)}) async-start(bf16[32,32,24,128]{3,2,1,0:T(8,128)(2,1)} %stack.2), calls=%async_computation | async-start | bytes 12582912 | tf_op jit(solution)/shard_map/all_to_all | solution.py:83
  30.8 3.9 %copy-start.11 = (bf16[32,16,128]{2,1,0:T(8,128)(2,1)S(1)}, bf16[32,16,128]{2,1,0:T(8,128)(2,1)}, u32[]{:S(2)}) copy-start(bf16[32,16,128]{2,1,0:T(8,128)(2,1)} %param.14) | copy-start | bytes 393220
  30.8 4.6 %copy-start.18 = (bf16[128,128]{1,0:T(8,128)(2,1)S(1)}, bf16[128,128]{1,0:T(8,128)(2,1)}, u32[]{:S(2)}) copy-start(bf16[128,128]{1,0:T(8,128)(2,1)} %param.18) | copy-start | bytes 98308
  30.8 112.9 %all-gather.2.cloned.1.call-start = ((), (), s32[]{:S(2)}) async-start(), calls=%async_computation.5 | async-start | bytes 3538944 | tf_op jit(solution)/shard_map/all_gather | solution.py:91
  31.7 4.1 %copy-start.13 = (bf16[32,16,128]{2,1,0:T(8,128)(2,1)S(1)}, bf16[32,16,128]{2,1,0:T(8,128)(2,1)}, u32[]{:S(2)}) copy-start(bf16[32,16,128]{2,1,0:T(8,128)(2,1)} %param.15) | copy-start | bytes 393220
  31.7 4.1 %copy-start.15 = (bf16[128,128]{1,0:T(8,128)(2,1)S(1)}, bf16[128,128]{1,0:T(8,128)(2,1)}, u32[]{:S(2)}) copy-start(bf16[128,128]{1,0:T(8,128)(2,1)} %param.19) | copy-start | bytes 98308
  32.4 1.2 copy-start.1
  34.5 269.6 %reduce-scatter.6.cloned.1.call-start = ((), (), s32[]{:S(2)}) async-start(), calls=%async_computation.6 | async-start | bytes 7864320 | tf_op jit(solution)/shard_map/reduce_scatter | solution.py:14
  187.1 4.8 %copy-start.3 = (f32[32,16,128]{0,1,2:T(8,128)S(1)}, f32[32,16,128]{0,1,2:T(8,128)}, u32[]{:S(2)}) copy-start(f32[32,16,128]{0,1,2:T(8,128)} %copy.79) | copy-start | bytes 786436
  187.1 4.9 %copy-start.23 = (f32[128]{0:T(128)S(1)}, f32[128]{0:T(128)}, u32[]{:S(2)}) copy-start(f32[128]{0:T(128)} %param.22) | copy-start | bytes 1540
  191.7 0.7 copy-start.24
  193.7 0.8 copy-start.8
  216.5 87.9 %copy-start.10 = (bf16[32,16,128]{0,1,2:T(8,128)(2,1)S(1)}, bf16[32,16,128]{0,1,2:T(8,128)(2,1)}, u32[]{:S(2)}) copy-start(bf16[32,16,128]{0,1,2:T(8,128)(2,1)} %get-tuple-element.15) | copy-start | bytes 393220
  216.5 88.4 %copy-start.16 = (bf16[128,128]{1,0:T(8,128)(2,1)S(1)}, bf16[128,128]{1,0:T(8,128)(2,1)}, u32[]{:S(2)}) copy-start(bf16[128,128]{1,0:T(8,128)(2,1)} %param.19) | copy-start | bytes 98308
  216.5 89.3 %copy-start.12 = (bf16[32,16,128]{2,1,0:T(8,128)(2,1)S(1)}, bf16[32,16,128]{2,1,0:T(8,128)(2,1)}, u32[]{:S(2)}) copy-start(bf16[32,16,128]{2,1,0:T(8,128)(2,1)} %param.14) | copy-start | bytes 393220
  216.5 89.3 %copy-start.14 = (bf16[32,16,128]{2,1,0:T(8,128)(2,1)S(1)}, bf16[32,16,128]{2,1,0:T(8,128)(2,1)}, u32[]{:S(2)}) copy-start(bf16[32,16,128]{2,1,0:T(8,128)(2,1)} %param.15) | copy-start | bytes 393220
  216.5 89.3 %copy-start.19 = (bf16[128,128]{1,0:T(8,128)(2,1)S(1)}, bf16[128,128]{1,0:T(8,128)(2,1)}, u32[]{:S(2)}) copy-start(bf16[128,128]{1,0:T(8,128)(2,1)} %param.18) | copy-start | bytes 98308
  216.5 89.2 %copy-start.21 = (f32[128]{0:T(128)S(1)}, f32[128]{0:T(128)}, u32[]{:S(2)}) copy-start(f32[128]{0:T(128)} %param.20) | copy-start | bytes 1540
  216.6 110.7 %all-to-all-start.1 = ((bf16[8,96,16,128]{3,2,1,0:T(8,128)(2,1)}), bf16[8,96,16,128]{3,2,1,0:T(8,128)(2,1)}, u32[]{:S(2)}, u32[]{:S(2)}) async-start(bf16[8,96,16,128]{3,2,1,0:T(8,128)(2,1)} %bitcast.79), calls=%async_computation.3 | async-start | bytes 6291456 | tf_op jit(solution)/shard_map/all_to_all | solution.py:25
  256.6 77.3 %reduce-scatter.8.cloned.1.call-start = ((), (), s32[]{:S(2)}) async-start(), calls=%async_computation.7 | async-start | bytes 1966080 | tf_op jit(solution)/shard_map/reduce_scatter | solution.py:14
  304.1 59.3 %reduce-scatter.10.cloned.1.call-start = ((), (), s32[]{:S(2)}) async-start(), calls=%async_computation.8 | async-start | bytes 589824
  304.9 24.8 %copy-start.2 = (f32[16,96,256]{2,1,0:T(8,128)S(1)}, f32[16,96,256]{2,1,0:T(8,128)}, u32[]{:S(2)}) copy-start(f32[16,96,256]{2,1,0:T(8,128)} %copy-done.1) | copy-start | bytes 4718596
  329.7 6.1 %copy-start.7 = (bf16[16,96,128]{2,1,0:T(8,128)(2,1)S(1)}, bf16[16,96,128]{2,1,0:T(8,128)(2,1)}, u32[]{:S(2)}) copy-start(bf16[16,96,128]{2,1,0:T(8,128)(2,1)} %param.13) | copy-start | bytes 1179652
  330.2 33.3 %copy-start.5 = (f32[32,24,256]{2,1,0:T(8,128)S(1)}, f32[32,24,256]{2,1,0:T(8,128)}, u32[]{:S(2)}) copy-start(f32[32,24,256]{2,1,0:T(8,128)} %copy-done.4) | copy-start | bytes 2359300
  335.8 28.8 %copy-start.9 = (bf16[32,24,128]{2,1,0:T(8,128)(2,1)S(1)}, bf16[32,24,128]{2,1,0:T(8,128)(2,1)}, u32[]{:S(2)}) copy-start(bf16[32,24,128]{2,1,0:T(8,128)(2,1)} %param.12) | copy-start | bytes 589828
  335.8 28.8 %copy-start.17 = (bf16[128,256]{1,0:T(8,128)(2,1)S(1)}, bf16[128,256]{1,0:T(8,128)(2,1)}, u32[]{:S(2)}) copy-start(bf16[128,256]{1,0:T(8,128)(2,1)} %param.16) | copy-start | bytes 196612
Sparse Core Ops, SparseCore 0:
  34.6 109.0 all-gather.1
  208.7 95.3 reduce-scatter.5
  306.7 27.1 reduce-scatter.7
  336.2 27.2 reduce-scatter.9
